TPU v7x, 32 devices: a whole 2x2x4 slice. The times are simulated.
32 devices in a mesh: dp: 16 (over z, y, core), tensor: 2 (over x).
Axes of the slice: x: 2, y: 2, z: 4, core: 2. Of those that a mesh axis runs over, the one named last changes fastest.
Arguments:
- tokens: float32 [11264, 2048], P(('dp', 'tensor')), may hold values from -6 to 6
- cotangent: float32 [11264, 2048], P(('dp', 'tensor')), may hold values from -6 to 6
- lengths: int32 [16, 13], P('dp'), may hold values from 1 to 176, 704 in all within a row
- parents: int32 [16, 13], P('dp'), may hold values from 0 to 11, as said below
- query_proj: float32 [2048, 2048], P('dp', 'tensor'), may hold values from -0.125 to 0.125
- key_proj: float32 [2048, 2048], P('dp', 'tensor'), may hold values from -0.125 to 0.125
- value_proj: float32 [2048, 2048], P('dp', 'tensor'), may hold values from -0.125 to 0.125
- out_proj: float32 [2048, 2048], P('tensor', 'dp'), may hold values from -0.375 to 0.375
- up_proj: float32 [2048, 8192], P('dp', 'tensor'), may hold values from -0.125 to 0.125
- down_proj: float32 [8192, 2048], P('tensor', 'dp'), may hold values from -0.0625 to 0.0625
- first_gain: float32 [2048], P(('dp', 'tensor')), may hold values from 0.5 to 1.5
- first_shift: float32 [2048], P(('dp', 'tensor')), may hold values from -3 to 3
- query_bias: float32 [2048], P(('dp', 'tensor')), may hold values from -3 to 3
- value_bias: float32 [2048], P(('dp', 'tensor')), may hold values from -3 to 3
- out_bias: float32 [2048], P(('dp', 'tensor')), may hold values from -3 to 3
- second_gain: float32 [2048], P(('dp', 'tensor')), may hold values from 0.5 to 1.5
- second_shift: float32 [2048], P(('dp', 'tensor')), may hold values from -3 to 3
- up_bias: float32 [8192], P(('dp', 'tensor')), may hold values from -3 to 3
- down_bias: float32 [2048], P(('dp', 'tensor')), may hold values from -3 to 3
Outputs:
- layer_output: float32 [11264, 2048], P(('dp', 'tensor'))
- tokens_grad: float32 [11264, 2048], P(('dp', 'tensor'))
- query_proj_grad: float32 [2048, 2048], P('dp', 'tensor')
- key_proj_grad: float32 [2048, 2048], P('dp', 'tensor')
- value_proj_grad: float32 [2048, 2048], P('dp', 'tensor')
- out_proj_grad: float32 [2048, 2048], P('tensor', 'dp')
- up_proj_grad: float32 [2048, 8192], P('dp', 'tensor')
- down_proj_grad: float32 [8192, 2048], P('tensor', 'dp')
- first_gain_grad: float32 [2048], P(('dp', 'tensor'))
- first_shift_grad: float32 [2048], P(('dp', 'tensor'))
- query_bias_grad: float32 [2048], P(('dp', 'tensor'))
- value_bias_grad: float32 [2048], P(('dp', 'tensor'))
- out_bias_grad: float32 [2048], P(('dp', 'tensor'))
- second_gain_grad: float32 [2048], P(('dp', 'tensor'))
- second_shift_grad: float32 [2048], P(('dp', 'tensor'))
- up_bias_grad: float32 [8192], P(('dp', 'tensor'))
- down_bias_grad: float32 [2048], P(('dp', 'tensor'))
Inputs may be any that keep to these rules, and one draw needn't show every extreme that they name: parents[t, 0] is 0 and parents[t, s] < s for s >= 1, so every segment follows its parent, and segment 0 is each tree's root; the last segment's parent is segment 13 - 2 in every tree. `lengths`: each row sums to 704, and its largest entry is exactly 176.
All inputs are finite; a program needn't handle non-finite values.
Results may differ from a plain program's by a relative error of at most 0.013.
Values may be sent and summed in bfloat16 or wider, within the bound.
No kernel may reach another device: no remote copies, remote signals or barrier semaphores. Data moves between devices by JAX's collectives and lax.ppermute only.
A program may use at most 384 MiB of HBM per device.

v0:
```python
import jax
import jax.numpy as jnp
from jax import lax
from jax.sharding import PartitionSpec as P

HEAD = 128
EPSILON = 1e-05
CONTRACT_ROWS = (((0,), (0,)), ((), ()))
CONTRACT_COLS = (((1,), (1,)), ((), ()))


def layer_norm(values, gain, shift):
    row_mean = jnp.mean(values, axis=-1, keepdims=True)
    centred = values - row_mean
    spread = jnp.mean(centred * centred, axis=-1, keepdims=True)
    return centred * lax.rsqrt(spread + EPSILON) * gain + shift


def exact_gelu(values):
    return jax.nn.gelu(values, approximate=False)


def tree_mask(seg_lengths, seg_parents, total):
    count = seg_lengths.shape[0]
    index = jnp.arange(count, dtype=jnp.int32)
    places = jnp.arange(total, dtype=jnp.int32)
    ends = jnp.cumsum(seg_lengths)
    segment = jnp.sum((places[:, None] >= ends[None, :]).astype(jnp.int32), axis=1)
    link = ((seg_parents[:, None] == index[None, :]) & (index[:, None] > 0)).astype(jnp.float32)
    identity = jnp.eye(count, dtype=jnp.float32)
    ancestry = lax.fori_loop(
        0, count, lambda step, held: jnp.maximum(identity, jnp.dot(link, held)), identity
    )
    onehot = (segment[:, None] == index[None, :]).astype(jnp.float32)
    reach = jnp.dot(jnp.dot(onehot, ancestry), onehot.T) > 0.5
    return reach & (places[None, :] <= places[:, None])


def masked_scores(query3, key3, allowed, scale):
    scaled = jnp.einsum("qhd,khd->hqk", query3, key3, preferred_element_type=jnp.float32) * scale
    return jnp.where(allowed[None], scaled, -jnp.inf)


def gather_rows(values):
    return lax.all_gather(values, "tensor", axis=0, tiled=True)


def sum_rows(values):
    return lax.psum_scatter(values, "tensor", scatter_dimension=0, tiled=True)


def column_sums(values):
    return jnp.sum(values.astype(jnp.float32), axis=0)


def local(
    tokens,
    cotangent,
    lengths,
    parents,
    query_proj,
    key_proj,
    value_proj,
    out_proj,
    up_proj,
    down_proj,
    first_gain,
    first_shift,
    query_bias,
    value_bias,
    out_bias,
    second_gain,
    second_shift,
    up_bias,
    down_bias,
):
    vectors = (
        lax.all_gather(first_gain, ("dp", "tensor"), axis=0, tiled=True),
        lax.all_gather(first_shift, ("dp", "tensor"), axis=0, tiled=True),
        lax.all_gather(query_bias, ("dp", "tensor"), axis=0, tiled=True),
        lax.all_gather(value_bias, ("dp", "tensor"), axis=0, tiled=True),
        lax.all_gather(out_bias, ("dp", "tensor"), axis=0, tiled=True),
        lax.all_gather(second_gain, ("dp", "tensor"), axis=0, tiled=True),
        lax.all_gather(second_shift, ("dp", "tensor"), axis=0, tiled=True),
        lax.all_gather(up_bias, ("dp", "tensor"), axis=0, tiled=True),
        lax.all_gather(down_bias, ("dp", "tensor"), axis=0, tiled=True),
    )
    (
        gain_one,
        shift_one,
        query_full,
        value_full,
        out_full,
        gain_two,
        shift_two,
        up_full,
        down_full,
    ) = vectors
    part = lax.axis_index("tensor")
    model_width = tokens.shape[1]
    width = query_proj.shape[1]
    hidden = up_proj.shape[1]
    heads_local = width // HEAD
    scale = HEAD ** (-0.5)
    query_local = lax.dynamic_slice_in_dim(query_full, part * width, width)
    value_local = lax.dynamic_slice_in_dim(value_full, part * width, width)
    up_local = lax.dynamic_slice_in_dim(up_full, part * hidden, hidden)
    attn_mats = (
        lax.all_gather(query_proj.astype(jnp.bfloat16), "dp", axis=0, tiled=True),
        lax.all_gather(key_proj.astype(jnp.bfloat16), "dp", axis=0, tiled=True),
        lax.all_gather(value_proj.astype(jnp.bfloat16), "dp", axis=0, tiled=True),
        lax.all_gather(out_proj.astype(jnp.bfloat16), "dp", axis=1, tiled=True),
    )
    ffwd_mats = (
        lax.all_gather(up_proj.astype(jnp.bfloat16), "dp", axis=0, tiled=True),
        lax.all_gather(down_proj.astype(jnp.bfloat16), "dp", axis=1, tiled=True),
    )
    w_query, w_key, w_value, w_out = attn_mats
    w_up, w_down = ffwd_mats
    first_norm, pull_first = jax.vjp(layer_norm, tokens, gain_one, shift_one)
    attn_in = gather_rows(first_norm.astype(jnp.bfloat16))
    total = attn_in.shape[0]
    queries = (jnp.dot(attn_in, w_query, preferred_element_type=jnp.float32) + query_local).astype(
        jnp.bfloat16
    )
    key_rows = jnp.dot(attn_in, w_key, preferred_element_type=jnp.float32).astype(jnp.bfloat16)
    value_rows = (
        jnp.dot(attn_in, w_value, preferred_element_type=jnp.float32) + value_local
    ).astype(jnp.bfloat16)
    query3 = queries.reshape(total, heads_local, HEAD)
    key3 = key_rows.reshape(total, heads_local, HEAD)
    value3 = value_rows.reshape(total, heads_local, HEAD)
    allowed = tree_mask(lengths[0], parents[0], total)
    scores = masked_scores(query3, key3, allowed, scale)
    top = jnp.max(scores, axis=-1, keepdims=True)
    log_total = top + jnp.log(jnp.sum(jnp.exp(scores - top), axis=-1, keepdims=True))
    probs = jnp.exp(scores - log_total)
    mixed = jnp.einsum(
        "hqk,khd->qhd", probs.astype(jnp.bfloat16), value3, preferred_element_type=jnp.float32
    )
    mixed_rows = mixed.reshape(total, width).astype(jnp.bfloat16)
    attn_part = jnp.dot(mixed_rows, w_out, preferred_element_type=jnp.float32)
    middle = tokens + sum_rows(attn_part) + out_full
    second_norm, pull_second = jax.vjp(layer_norm, middle, gain_two, shift_two)
    ffwd_in = gather_rows(second_norm.astype(jnp.bfloat16))
    pre_act = jnp.dot(ffwd_in, w_up, preferred_element_type=jnp.float32) + up_local
    activ, pull_gelu = jax.vjp(exact_gelu, pre_act)
    act_rows = activ.astype(jnp.bfloat16)
    ffwd_part = jnp.dot(act_rows, w_down, preferred_element_type=jnp.float32)
    layer_output = middle + sum_rows(ffwd_part) + down_full
    down_cot = cotangent.astype(jnp.bfloat16)
    down_bias_grad = column_sums(down_cot)
    down_all = gather_rows(down_cot)
    act_grad = lax.dot_general(down_all, w_down, CONTRACT_COLS, preferred_element_type=jnp.float32)
    (pre_grad,) = pull_gelu(act_grad)
    pre_rows = pre_grad.astype(jnp.bfloat16)
    up_bias_grad = column_sums(pre_rows)
    second_in = lax.dot_general(pre_rows, w_up, CONTRACT_COLS, preferred_element_type=jnp.float32)
    in_cols = ffwd_in
    cot_cols = down_all
    up_term = lax.dot_general(in_cols, pre_rows, CONTRACT_ROWS, preferred_element_type=jnp.float32)
    down_term = lax.dot_general(
        cot_cols, act_rows, CONTRACT_ROWS, preferred_element_type=jnp.float32
    )
    ffwd_sum = lax.psum_scatter(
        jnp.concatenate([up_term, down_term], axis=1), "dp", scatter_dimension=0, tiled=True
    )
    middle_part, gain_two_grad, shift_two_grad = pull_second(sum_rows(second_in))
    middle_grad = cotangent + middle_part
    attn_cot = middle_grad.astype(jnp.bfloat16)
    out_bias_grad = column_sums(attn_cot)
    attn_all = gather_rows(attn_cot)
    mixed_grad = lax.dot_general(
        attn_all, w_out, CONTRACT_COLS, preferred_element_type=jnp.float32
    ).astype(jnp.bfloat16)
    grad3 = mixed_grad.reshape(total, heads_local, HEAD)
    again = jnp.exp(masked_scores(query3, key3, allowed, scale) - log_total)
    value_part = jnp.einsum(
        "hqk,qhd->khd", again.astype(jnp.bfloat16), grad3, preferred_element_type=jnp.float32
    )
    prob_grad = jnp.einsum("qhd,khd->hqk", grad3, value3, preferred_element_type=jnp.float32)
    row_inner = jnp.sum(again * prob_grad, axis=-1, keepdims=True)
    score_grad = (again * (prob_grad - row_inner)).astype(jnp.bfloat16)
    query_grad = (
        (jnp.einsum("hqk,khd->qhd", score_grad, key3, preferred_element_type=jnp.float32) * scale)
        .reshape(total, width)
        .astype(jnp.bfloat16)
    )
    key_grad = (
        (jnp.einsum("hqk,qhd->khd", score_grad, query3, preferred_element_type=jnp.float32) * scale)
        .reshape(total, width)
        .astype(jnp.bfloat16)
    )
    value_grad = value_part.reshape(total, width).astype(jnp.bfloat16)
    query_bias_part = column_sums(query_grad)
    value_bias_part = column_sums(value_grad)
    stacked = jnp.concatenate([query_grad, key_grad, value_grad], axis=1)
    first_in = lax.dot_general(
        query_grad, w_query, CONTRACT_COLS, preferred_element_type=jnp.float32
    )
    first_in = first_in + lax.dot_general(
        key_grad, w_key, CONTRACT_COLS, preferred_element_type=jnp.float32
    )
    first_in = first_in + lax.dot_general(
        value_grad, w_value, CONTRACT_COLS, preferred_element_type=jnp.float32
    )
    in_cols = attn_in
    cot_cols = attn_all
    proj_term = lax.dot_general(in_cols, stacked, CONTRACT_ROWS, preferred_element_type=jnp.float32)
    out_term = lax.dot_general(
        cot_cols, mixed_rows, CONTRACT_ROWS, preferred_element_type=jnp.float32
    )
    attn_sum = lax.psum_scatter(
        jnp.concatenate([proj_term, out_term], axis=1), "dp", scatter_dimension=0, tiled=True
    )
    tokens_part, gain_one_grad, shift_one_grad = pull_first(sum_rows(first_in))
    tokens_grad = middle_grad + tokens_part
    zeros_model = jnp.zeros((model_width,), jnp.float32)
    query_bias_full = lax.dynamic_update_slice_in_dim(zeros_model, query_bias_part, part * width, 0)
    value_bias_full = lax.dynamic_update_slice_in_dim(zeros_model, value_bias_part, part * width, 0)
    up_bias_full = lax.dynamic_update_slice_in_dim(
        jnp.zeros((up_full.shape[0],), jnp.float32), up_bias_grad, part * hidden, 0
    )
    vector_grads = (
        lax.psum_scatter(gain_one_grad, ("dp", "tensor"), scatter_dimension=0, tiled=True),
        lax.psum_scatter(shift_one_grad, ("dp", "tensor"), scatter_dimension=0, tiled=True),
        lax.psum_scatter(query_bias_full, ("dp", "tensor"), scatter_dimension=0, tiled=True),
        lax.psum_scatter(value_bias_full, ("dp", "tensor"), scatter_dimension=0, tiled=True),
        lax.psum_scatter(out_bias_grad, ("dp", "tensor"), scatter_dimension=0, tiled=True),
        lax.psum_scatter(gain_two_grad, ("dp", "tensor"), scatter_dimension=0, tiled=True),
        lax.psum_scatter(shift_two_grad, ("dp", "tensor"), scatter_dimension=0, tiled=True),
        lax.psum_scatter(up_bias_full, ("dp", "tensor"), scatter_dimension=0, tiled=True),
        lax.psum_scatter(down_bias_grad, ("dp", "tensor"), scatter_dimension=0, tiled=True),
    )
    query_proj_grad = attn_sum[:, :width]
    key_proj_grad = attn_sum[:, width : 2 * width]
    value_proj_grad = attn_sum[:, 2 * width : 3 * width]
    out_proj_grad = attn_sum[:, 3 * width :].T
    up_proj_grad = ffwd_sum[:, :hidden]
    down_proj_grad = ffwd_sum[:, hidden:].T
    return (
        layer_output,
        tokens_grad,
        query_proj_grad,
        key_proj_grad,
        value_proj_grad,
        out_proj_grad,
        up_proj_grad,
        down_proj_grad,
        vector_grads[0],
        vector_grads[1],
        vector_grads[2],
        vector_grads[3],
        vector_grads[4],
        vector_grads[5],
        vector_grads[6],
        vector_grads[7],
        vector_grads[8],
    )


def solution(mesh):
    placed = (
        P(("dp", "tensor"), None),
        P(("dp", "tensor"), None),
        P("dp", None),
        P("dp", None),
        P("dp", "tensor"),
        P("dp", "tensor"),
        P("dp", "tensor"),
        P("tensor", "dp"),
        P("dp", "tensor"),
        P("tensor", "dp"),
        P(("dp", "tensor")),
        P(("dp", "tensor")),
        P(("dp", "tensor")),
        P(("dp", "tensor")),
        P(("dp", "tensor")),
        P(("dp", "tensor")),
        P(("dp", "tensor")),
        P(("dp", "tensor")),
        P(("dp", "tensor")),
    )
    return jax.shard_map(
        local,
        mesh=mesh,
        in_specs=placed,
        out_specs=(
            P(("dp", "tensor"), None),
            P(("dp", "tensor"), None),
            P("dp", "tensor"),
            P("dp", "tensor"),
            P("dp", "tensor"),
            P("tensor", "dp"),
            P("dp", "tensor"),
            P("tensor", "dp"),
            P(("dp", "tensor")),
            P(("dp", "tensor")),
            P(("dp", "tensor")),
            P(("dp", "tensor")),
            P(("dp", "tensor")),
            P(("dp", "tensor")),
            P(("dp", "tensor")),
            P(("dp", "tensor")),
            P(("dp", "tensor")),
        ),
        check_vma=False,
    )
```

profile of v0, /device:TPU:0, one launch (start us, length us, event | category | flops | bytes accessed | tf_op | source)
XLA Modules:
  0.0 2250.7 jit_solution(2644074207018652300)
XLA Ops:
  12.3 42.6 %all-reduce.18 = (f32[2048]{0:T(1024)S(1)}, f32[2048]{0:T(1024)S(1)}, f32[2048]{0:T(1024)S(1)}, f32[2048]{0:T(1024)S(1)}, f32[2048]{0:T(1024)S(1)}, /*index=5*/f32[2048]{0:T(1024)S(1)}, f32[2048]{0:T(1024)S(1)}) all-reduce(f32[2048]{0:T(1024)S(1)} %dynamic-update-slice.1, ...), channel_id=1, replica_groups=mesh['dp'=16,'tensor'=2] {'dp','tensor'}, use_global_device_ids=true, to_apply=%add.1 | all-reduce | flops 14336 | bytes 114688
  70.2 28.4 %all-gather.12.cloned.1.call-done = bf16[704,2048]{1,0:T(8,128)(2,1)} async-done(((bf16[352,2048]{1,0:T(8,128)(2,1)}), bf16[704,2048]{1,0:T(8,128)(2,1)}) %all-gather.12.cloned.1.call-update) | async-done | bytes 2883600 | tf_op jit(solution)/shard_map/all_gather | solution.py:45
  98.6 53.3 %all-gather.18.cloned.1.call-done = bf16[2048,1024]{1,0:T(8,128)(2,1)} async-done(((bf16[128,1024]{1,0:T(8,128)(2,1)}), bf16[2048,1024]{1,0:T(8,128)(2,1)}) %all-gather.18.cloned.1.call-update) | async-done | bytes 4194320 | tf_op jit(solution)/shard_map/all_gather | solution.py:110
  159.2 44.4 %all-gather.16.cloned.1.call-done = bf16[2048,1024]{1,0:T(8,128)(2,1)} async-done(((bf16[128,1024]{1,0:T(8,128)(2,1)}), bf16[2048,1024]{1,0:T(8,128)(2,1)}) %all-gather.16.cloned.1.call-update) | async-done | bytes 4194320 | tf_op jit(solution)/shard_map/all_gather | solution.py:109
  227.9 27.2 %all-gather.14.cloned.1.call-done = bf16[2048,1024]{1,0:T(8,128)(2,1)} async-done(((bf16[128,1024]{1,0:T(8,128)(2,1)}), bf16[2048,1024]{1,0:T(8,128)(2,1)}) %all-gather.14.cloned.1.call-update) | async-done | bytes 4194320 | tf_op jit(solution)/shard_map/all_gather | solution.py:111
  274.9 33.9 %all-gather.20.cloned.1.call-done = bf16[1024,2048]{1,0:T(8,128)(2,1)} async-done(((bf16[1024,128]{1,0:T(8,128)(2,1)}), bf16[1024,2048]{1,0:T(8,128)(2,1)}) %all-gather.20.cloned.1.call-update) | async-done | bytes 4194320 | tf_op jit(solution)/shard_map/all_gather | solution.py:112
  317.3 69.7 %reduce-scatter.7.cloned.1.call-done = f32[352,2048]{1,0:T(8,128)} async-done(((f32[704,2048]{1,0:T(8,128)}), f32[352,2048]{1,0:T(8,128)}) %reduce-scatter.7.cloned.1.call-update) | async-done | bytes 2883600 | tf_op jit(solution)/shard_map/reduce_scatter | solution.py:49
  400.5 67.7 %all-gather = f32[32,1,256]{2,1,0:T(1,128)S(1)} all-gather(f32[1,1,256]{2,1,0:T(1,128)S(1)} %bitcast.124), channel_id=1, replica_groups=mesh['dp'=16,'tensor'=2] {'dp','tensor'}, dimensions={0}, use_global_device_ids=true | all-gather | bytes 33792 | tf_op jit(solution)/shard_map/all_gather | solution.py:85
  468.2 95.6 %all-gather.24.cloned.1.call-done = bf16[2048,4096]{1,0:T(8,128)(2,1)} async-done(((bf16[128,4096]{1,0:T(8,128)(2,1)}), bf16[2048,4096]{1,0:T(8,128)(2,1)}) %all-gather.24.cloned.1.call-update) | async-done | bytes 16777232 | tf_op jit(solution)/shard_map/all_gather | solution.py:115
  563.8 19.0 fusion.72
  582.7 22.8 %all-gather.28.cloned.1.call-done = bf16[704,2048]{1,0:T(8,128)(2,1)} async-done(((bf16[352,2048]{1,0:T(8,128)(2,1)}), bf16[704,2048]{1,0:T(8,128)(2,1)}) %all-gather.28.cloned.1.call-update) | async-done | bytes 2883600 | tf_op jit(solution)/shard_map/all_gather | solution.py:45
  605.5 131.9 %all-gather.26.cloned.1.call-done = bf16[4096,2048]{1,0:T(8,128)(2,1)} async-done(((bf16[4096,128]{1,0:T(8,128)(2,1)}), bf16[4096,2048]{1,0:T(8,128)(2,1)}) %all-gather.26.cloned.1.call-update) | async-done | bytes 16777232 | tf_op jit(solution)/shard_map/all_gather | solution.py:116
  737.4 43.0 %convert_reduce_fusion = (f32[4096]{0:T(1024)S(1)}, bf16[704,4096]{1,0:T(8,128)(2,1)S(1)}, f32[704,4096]{1,0:T(8,128)}) fusion(f32[704,4096]{1,0:T(8,128)} %fusion.72, f32[4096]{0:T(1024)S(1)} %dynamic_slice.11, bf16[704,2048]{1,0:T(8,128)(2,1)} %all-gather.28.cloned.1.call-done, bf16[4096,2048]{1,0:T(8,128)(2,1)} %all-gather.26.cloned.1.call-done), kind=kOutput, calls=%fused_computation.20 | convolution fusion | flops 12027424768 | bytes 48529408 | tf_op jit(solution)/shard_map/dot_general | solution.py:154
  800.5 69.7 %reduce-scatter.11.cloned.1.call-done = f32[352,2048]{1,0:T(8,128)} async-done(((f32[704,2048]{1,0:T(8,128)}), f32[352,2048]{1,0:T(8,128)}) %reduce-scatter.11.cloned.1.call-update) | async-done | bytes 2883600 | tf_op jit(solution)/shard_map/reduce_scatter | solution.py:49
  878.3 41.6 %all-gather.30.cloned.1.call-done = bf16[704,2048]{1,0:T(8,128)(2,1)} async-done(((bf16[352,2048]{1,0:T(8,128)(2,1)}), bf16[704,2048]{1,0:T(8,128)(2,1)}) %all-gather.30.cloned.1.call-update) | async-done | bytes 2883600 | tf_op jit(solution)/shard_map/all_gather | solution.py:45
  1000.1 58.3 %reduce-scatter.13.cloned.1.call-done = f32[352,2048]{1,0:T(8,128)} async-done(((f32[704,2048]{1,0:T(8,128)}), f32[352,2048]{1,0:T(8,128)}) %reduce-scatter.13.cloned.1.call-update) | async-done | bytes 2883600 | tf_op jit(solution)/shard_map/reduce_scatter | solution.py:49
  1061.9 18.9 fusion.73
  1104.9 23.2 %pad_maximum_fusion.1 = f32[2048,4096]{1,0:T(8,128)} fusion(f32[2048,1024]{1,0:T(8,128)} %fusion.30, f32[2048,3072]{1,0:T(8,128)} %fusion.17), kind=kLoop, calls=%fused_computation.10 | loop fusion | flops 8388608 | bytes 67108864 | tf_op jit(solution)/shard_map/concatenate | solution.py:214
  1128.2 22.9 %convolution_bitcast_fusion = f32[2048,4096]{1,0:T(8,128)} fusion(bf16[704,4096]{1,0:T(8,128)(2,1)} %multiply_convert_fusion.1, bf16[704,2048]{1,0:T(8,128)(2,1)} %all-gather.28.cloned.1.call-done), kind=kOutput, calls=%fused_computation.17 | convolution fusion | flops 11811160064 | bytes 42205184 | tf_op jit(solution)/shard_map/dot_general | solution.py:162
  1151.1 20.0 fusion.75
  1171.1 46.0 %pad_maximum_fusion = f32[2048,8192]{1,0:T(8,128)} fusion(f32[2048,4096]{1,0:T(8,128)} %convolution_bitcast_fusion, f32[2048,4096]{1,0:T(8,128)} %fusion.75), kind=kLoop, calls=%fused_computation.9 | loop fusion | flops 16777216 | bytes 134217728 | tf_op jit(solution)/shard_map/concatenate | solution.py:166
  1236.3 31.9 %reduce-scatter.9.cloned.1.call-done = f32[352,2048]{1,0:T(8,128)} async-done(((f32[704,2048]{1,0:T(8,128)}), f32[352,2048]{1,0:T(8,128)}) %reduce-scatter.9.cloned.1.call-update) | async-done | bytes 2883600 | tf_op jit(solution)/shard_map/reduce_scatter | solution.py:49
  1272.0 330.8 %reduce-scatter.15.cloned.1.call-done = f32[128,4096]{1,0:T(8,128)} async-done(((f32[2048,4096]{1,0:T(8,128)}), f32[128,4096]{1,0:T(8,128)}) %reduce-scatter.15.cloned.1.call-update) | async-done | bytes 2097168 | tf_op jit(solution)/shard_map/reduce_scatter | solution.py:213
  1606.5 631.8 %reduce-scatter.17.cloned.1.call-done = f32[128,8192]{1,0:T(8,128)} async-done(((f32[2048,8192]{1,0:T(8,128)}), f32[128,8192]{1,0:T(8,128)}) %reduce-scatter.17.cloned.1.call-update) | async-done | bytes 4194320 | tf_op jit(solution)/shard_map/reduce_scatter | solution.py:165
  (306 shorter events, 263.6 us)
Async XLA Ops:
  7.3 91.4 %all-gather.12.cloned.1.call-start = ((), (), s32[]{:S(2)}) async-start(), calls=%async_computation.6 | async-start | bytes 4325376 | tf_op jit(solution)/shard_map/all_gather | solution.py:45
  54.9 334.9 %copy-start.30 = (f32[2048]{0:T(1024)}, f32[2048]{0:T(1024)S(1)}, u32[]{:S(2)}) copy-start(f32[2048]{0:T(1024)S(1)} %get-tuple-element.151) | copy-start | bytes 24580
  56.7 95.3 %all-gather.18.cloned.1.call-start = ((), (), s32[]{:S(2)}) async-start(), calls=%async_computation.9 | async-start | bytes 4456448 | tf_op jit(solution)/shard_map/all_gather | solution.py:110
  57.5 146.1 %all-gather.16.cloned.1.call-start = ((), (), s32[]{:S(2)}) async-start(), calls=%async_computation.8 | async-start | bytes 4456448 | tf_op jit(solution)/shard_map/all_gather | solution.py:109
  59.3 195.8 %all-gather.14.cloned.1.call-start = ((), (), s32[]{:S(2)}) async-start(), calls=%async_computation.7 | async-start | bytes 4456448 | tf_op jit(solution)/shard_map/all_gather | solution.py:111
  61.2 247.6 %all-gather.20.cloned.1.call-start = ((), (), s32[]{:S(2)}) async-start(), calls=%async_computation.10 | async-start | bytes 4456448 | tf_op jit(solution)/shard_map/all_gather | solution.py:112
  63.0 324.0 %reduce-scatter.7.cloned.1.call-start = ((), (), s32[]{:S(2)}) async-start(), calls=%async_computation.11 | async-start | bytes 8650752 | tf_op jit(solution)/shard_map/reduce_scatter | solution.py:49
  70.2 191.2 %copy-start.12 = (pred[704,704]{0,1:T(8,128)(4,1)}, pred[704,704]{0,1:T(8,128)(4,1)S(1)}, u32[]{:S(2)}) copy-start(pred[704,704]{0,1:T(8,128)(4,1)S(1)} %copy.89) | copy-start | bytes 1486852
  317.3 150.9 %all-gather.22.cloned.1.call-start = ((), (), s32[]{:S(2)}) async-start(), calls=%async_computation.12 | async-start | bytes 4325376 | tf_op jit(solution)/shard_map/all_gather | solution.py:45
  392.6 171.2 %all-gather.24.cloned.1.call-start = ((), (), s32[]{:S(2)}) async-start(), calls=%async_computation.13 | async-start | bytes 17825792 | tf_op jit(solution)/shard_map/all_gather | solution.py:115
  395.4 210.1 %all-gather.28.cloned.1.call-start = ((), (), s32[]{:S(2)}) async-start(), calls=%async_computation.16 | async-start | bytes 4325376 | tf_op jit(solution)/shard_map/all_gather | solution.py:45
  397.4 340.0 %all-gather.26.cloned.1.call-start = ((), (), s32[]{:S(2)}) async-start(), calls=%async_computation.14 | async-start | bytes 17825792 | tf_op jit(solution)/shard_map/all_gather | solution.py:116
  400.4 469.8 %reduce-scatter.11.cloned.1.call-start = ((), (), s32[]{:S(2)}) async-start(), calls=%async_computation.17 | async-start | bytes 8650752 | tf_op jit(solution)/shard_map/reduce_scatter | solution.py:49
  800.4 73.4 %copy-start.48 = (f32[352]{0:T(512)S(1)}, f32[352]{0:T(512)}, u32[]{:S(2)}) copy-start(f32[352]{0:T(512)} %copy-done.47) | copy-start | bytes 4228
  800.5 119.5 %all-gather.30.cloned.1.call-start = ((), (), s32[]{:S(2)}) async-start(), calls=%async_computation.18 | async-start | bytes 4325376 | tf_op jit(solution)/shard_map/all_gather | solution.py:45
  877.8 180.6 %reduce-scatter.13.cloned.1.call-start = ((), (), s32[]{:S(2)}) async-start(), calls=%async_computation.19 | async-start | bytes 8650752 | tf_op jit(solution)/shard_map/reduce_scatter | solution.py:49
  986.8 238.0 %all-reduce.21.cloned.1.call-start = ((), (), s32[]{:S(2)}) async-start(), calls=%async_computation.22 | async-start | bytes 212992
  988.1 70.4 %copy-start.1 = (f32[352,2048]{1,0:T(8,128)S(1)}, f32[352,2048]{1,0:T(8,128)}, u32[]{:S(2)}) copy-start(f32[352,2048]{1,0:T(8,128)} %param.21) | copy-start | bytes 8650756
  988.1 70.4 %copy-start.28 = (f32[2048]{0:T(1024)S(1)}, f32[2048]{0:T(1024)}, u32[]{:S(2)}) copy-start(f32[2048]{0:T(1024)} %copy-done.27) | copy-start | bytes 24580
  988.1 70.3 %copy-start.33 = (f32[352]{0:T(512)S(1)}, f32[352]{0:T(512)}, u32[]{:S(2)}) copy-start(f32[352]{0:T(512)} %copy-done.32) | copy-start | bytes 4228
  988.1 70.3 %copy-start.41 = (f32[352]{0:T(512)S(1)}, f32[352]{0:T(512)}, u32[]{:S(2)}) copy-start(f32[352]{0:T(512)} %copy-done.40) | copy-start | bytes 4228
  1061.9 206.2 %reduce-scatter.9.cloned.1.call-start = ((), (), s32[]{:S(2)}) async-start(), calls=%async_computation.15 | async-start | bytes 8650752 | tf_op jit(solution)/shard_map/reduce_scatter | solution.py:49
  1080.9 521.9 %reduce-scatter.15.cloned.1.call-start = ((), (), s32[]{:S(2)}) async-start(), calls=%async_computation.20 | async-start | bytes 35651584 | tf_op jit(solution)/shard_map/reduce_scatter | solution.py:213
  1128.1 1110.1 %reduce-scatter.17.cloned.1.call-start = ((), (), s32[]{:S(2)}) async-start(), calls=%async_computation.21 | async-start | bytes 71303168 | tf_op jit(solution)/shard_map/reduce_scatter | solution.py:165
  (67 other events, 974.5 us)
Sparse Core Ops, SparseCore 0:
  56.8 41.8 all-gather.11
  101.4 50.5 all-gather.17
  154.7 48.9 all-gather.15
  206.2 48.9 all-gather.13
  257.8 50.9 all-gather.19
  317.4 69.6 reduce-scatter.6
  392.7 42.3 all-gather.21
  437.2 126.4 all-gather.23
  565.3 40.1 all-gather.27
  607.5 129.8 all-gather.25
  800.6 69.6 reduce-scatter.10
  877.9 41.9 all-gather.29
  987.0 71.4 reduce-scatter.12
  1065.3 128.1 all-reduce.20
  1195.6 72.4 reduce-scatter.8
  1272.2 330.5 reduce-scatter.14
  1606.9 631.3 reduce-scatter.16
where the time goes:
time: 2260 us; the launch traced here: 2250 us
  waiting for transfers between devices  1670 us (74%)
  matrix products  267 us (12%)
  other arithmetic  145 us (6%)
  blocking collectives  110 us (5%)
  local copies, waits for them, and re-layouts  40.6 us (2%)
    reduce_scatter x1, waiting for transfers between devices, local(): lax.psum_scatter(jnp.concatenate([up_term, down_term], axis=1), 'dp', sca...  632 us
    reduce_scatter x1, waiting for transfers between devices, local(): lax.psum_scatter(jnp.concatenate([proj_term, out_term], axis=1), 'dp', sc...  331 us
    reduce_scatter x4, waiting for transfers between devices, sum_rows(): return lax.psum_scatter(values, 'tensor', scatter_dimension=0, tiled=True)  230 us
    all_gather x1, waiting for transfers between devices, local(): lax.all_gather(down_proj.astype(jnp.bfloat16), 'dp', axis=1, tiled=True)  132 us
    all_gather x1, waiting for transfers between devices, local(): lax.all_gather(up_proj.astype(jnp.bfloat16), 'dp', axis=0, tiled=True)  95.6 us
    all_gather x4, waiting for transfers between devices, gather_rows(): return lax.all_gather(values, 'tensor', axis=0, tiled=True)  92.8 us
    all_gather x1, blocking collectives, local(): lax.all_gather(up_bias, ('dp', 'tensor'), axis=0, tiled=True)  67.7 us
    all_gather x1, waiting for transfers between devices, local(): lax.all_gather(key_proj.astype(jnp.bfloat16), 'dp', axis=0, tiled=True)  53.3 us
  transfers between devices with their start and end apart: 17, of which 15 were waited for; matrix products, arithmetic and copies ran while one was open for 12% of the time, Pallas kernels for 0%

commit v1 on v0

--- a/solution.py
+++ b/solution.py
@@ -7,6 +7,18 @@
 EPSILON = 1e-05
 CONTRACT_ROWS = (((0,), (0,)), ((), ()))
 CONTRACT_COLS = (((1,), (1,)), ((), ()))
+
+
+def gather_by_bits(array, axis, dim):
+    ways, here, hop = (lax.axis_size(axis), lax.axis_index(axis), array.shape[dim])
+    line, have = (array, 1)
+    while have < ways:
+        line = jnp.concatenate(
+            [line, lax.ppermute(line, axis, [(d, (d - have) % ways) for d in range(ways)])],
+            axis=dim,
+        )
+        have = 2 * have
+    return jnp.roll(line, here * hop, axis=dim)
 
 
 def layer_norm(values, gain, shift):
@@ -113,7 +125,7 @@
     )
     ffwd_mats = (
         lax.all_gather(up_proj.astype(jnp.bfloat16), "dp", axis=0, tiled=True),
-        lax.all_gather(down_proj.astype(jnp.bfloat16), "dp", axis=1, tiled=True),
+        gather_by_bits(down_proj.astype(jnp.bfloat16), "dp", 1),
     )
     w_query, w_key, w_value, w_out = attn_mats
     w_up, w_down = ffwd_mats

time: 2260 us -> 2630 us (1.16)
  blocking collectives: 110 us -> 325 us
  waiting for transfers between devices: 1670 us -> 1800 us
    ppermute x0 -> x4, waiting for transfers between devices: none -> 319 us  [gather_by_bits(): lax.ppermute(line, axis, [(d, (d - have) % ways) for d in range(ways)])]
    all_gather x1, blocking collectives: 67.7 us -> 282 us  [local(): lax.all_gather(up_bias, ('dp', 'tensor'), axis=0, tiled=True)]
    all_gather x1 -> x0, waiting for transfers between devices: 132 us -> none  [local(): lax.all_gather(down_proj.astype(jnp.bfloat16), 'dp', axis=1, tiled=True)]
    all_gather x1, waiting for transfers between devices: 95.6 us -> 0.01 us  [local(): lax.all_gather(up_proj.astype(jnp.bfloat16), 'dp', axis=0, tiled=True)]
    reduce_scatter x4, waiting for transfers between devices: 230 us -> 293 us  [sum_rows(): return lax.psum_scatter(values, 'tensor', scatter_dimension=0, tiled=True)]
  transfers between devices with their start and end apart: 17 -> 20, of which waited for: 15 -> 16; matrix products, arithmetic and copies ran while one was open for 12% -> 12% of each run, Pallas kernels for 0% -> 0%
where the time goes in v1:
time: 2630 us
  waiting for transfers between devices  1800 us (68%)
  blocking collectives  325 us (12%)
  matrix products  273 us (10%)
  other arithmetic  136 us (5%)
  local copies, waits for them, and re-layouts  66.6 us (3%)
    reduce_scatter x1, waiting for transfers between devices, local(): lax.psum_scatter(jnp.concatenate([up_term, down_term], axis=1), 'dp', sca...  632 us
    reduce_scatter x1, waiting for transfers between devices, local(): lax.psum_scatter(jnp.concatenate([proj_term, out_term], axis=1), 'dp', sc...  331 us
    ppermute x4, waiting for transfers between devices, gather_by_bits(): lax.ppermute(line, axis, [(d, (d - have) % ways) for d in range(ways)])  319 us
    reduce_scatter x4, waiting for transfers between devices, sum_rows(): return lax.psum_scatter(values, 'tensor', scatter_dimension=0, tiled=True)  293 us
    all_gather x1, blocking collectives, local(): lax.all_gather(up_bias, ('dp', 'tensor'), axis=0, tiled=True)  282 us
    all_gather x4, waiting for transfers between devices, gather_rows(): return lax.all_gather(values, 'tensor', axis=0, tiled=True)  70.4 us
    all_gather x1, waiting for transfers between devices, local(): lax.all_gather(key_proj.astype(jnp.bfloat16), 'dp', axis=0, tiled=True)  53.3 us
  transfers between devices with their start and end apart: 20, of which 16 were waited for; matrix products, arithmetic and copies ran while one was open for 12% of the time, Pallas kernels for 0%

profile of v1, /device:TPU:0, one launch (start us, length us, event | category | flops | bytes accessed | tf_op | source)
XLA Modules:
  0.0 2627.1 jit_solution(15787195844359170320)
XLA Ops:
  12.3 42.6 %all-reduce.18 = (f32[2048]{0:T(1024)S(1)}, f32[2048]{0:T(1024)S(1)}, f32[2048]{0:T(1024)S(1)}, f32[2048]{0:T(1024)S(1)}, f32[2048]{0:T(1024)S(1)}, /*index=5*/f32[2048]{0:T(1024)S(1)}, f32[2048]{0:T(1024)S(1)}) all-reduce(f32[2048]{0:T(1024)S(1)} %dynamic-update-slice.1, ...), channel_id=1, replica_groups=mesh['dp'=16,'tensor'=2] {'dp','tensor'}, use_global_device_ids=true, to_apply=%add.1 | all-reduce | flops 14336 | bytes 114688
  70.3 28.4 %all-gather.11.cloned.1.call-done = bf16[704,2048]{1,0:T(8,128)(2,1)} async-done(((bf16[352,2048]{1,0:T(8,128)(2,1)}), bf16[704,2048]{1,0:T(8,128)(2,1)}) %all-gather.11.cloned.1.call-update) | async-done | bytes 2883600 | tf_op jit(solution)/shard_map/all_gather | solution.py:57
  98.6 53.3 %all-gather.17.cloned.1.call-done = bf16[2048,1024]{1,0:T(8,128)(2,1)} async-done(((bf16[128,1024]{1,0:T(8,128)(2,1)}), bf16[2048,1024]{1,0:T(8,128)(2,1)}) %all-gather.17.cloned.1.call-update) | async-done | bytes 4194320 | tf_op jit(solution)/shard_map/all_gather | solution.py:122
  159.2 44.4 %all-gather.15.cloned.1.call-done = bf16[2048,1024]{1,0:T(8,128)(2,1)} async-done(((bf16[128,1024]{1,0:T(8,128)(2,1)}), bf16[2048,1024]{1,0:T(8,128)(2,1)}) %all-gather.15.cloned.1.call-update) | async-done | bytes 4194320 | tf_op jit(solution)/shard_map/all_gather | solution.py:121
  227.6 27.5 %all-gather.13.cloned.1.call-done = bf16[2048,1024]{1,0:T(8,128)(2,1)} async-done(((bf16[128,1024]{1,0:T(8,128)(2,1)}), bf16[2048,1024]{1,0:T(8,128)(2,1)}) %all-gather.13.cloned.1.call-update) | async-done | bytes 4194320 | tf_op jit(solution)/shard_map/all_gather | solution.py:123
  274.8 33.9 %all-gather.19.cloned.1.call-done = bf16[1024,2048]{1,0:T(8,128)(2,1)} async-done(((bf16[1024,128]{1,0:T(8,128)(2,1)}), bf16[1024,2048]{1,0:T(8,128)(2,1)}) %all-gather.19.cloned.1.call-update) | async-done | bytes 4194320 | tf_op jit(solution)/shard_map/all_gather | solution.py:124
  317.7 69.7 %reduce-scatter.7.cloned.1.call-done = f32[352,2048]{1,0:T(8,128)} async-done(((f32[704,2048]{1,0:T(8,128)}), f32[352,2048]{1,0:T(8,128)}) %reduce-scatter.7.cloned.1.call-update) | async-done | bytes 2883600 | tf_op jit(solution)/shard_map/reduce_scatter | solution.py:61
  413.9 56.8 %collective-permute-done.1 = bf16[4096,256]{1,0:T(8,128)(2,1)S(1)} collective-permute-done((bf16[4096,256]{1,0:T(8,128)(2,1)S(1)}, bf16[4096,256]{1,0:T(8,128)(2,1)S(1)}, u32[]{:S(2)}, u32[]{:S(2)}) %collective-permute-start.1) | collective-permute-done | bytes 2097184 | tf_op jit(solution)/shard_map/ppermute | solution.py:17
  471.2 110.6 %collective-permute-done.2 = bf16[4096,512]{1,0:T(8,128)(2,1)S(1)} collective-permute-done((bf16[4096,512]{1,0:T(8,128)(2,1)S(1)}, bf16[4096,512]{1,0:T(8,128)(2,1)S(1)}, u32[]{:S(2)}, u32[]{:S(2)}) %collective-permute-start.2) | collective-permute-done | bytes 4194336 | tf_op jit(solution)/shard_map/ppermute | solution.py:17
  588.7 282.4 %all-gather = f32[32,1,256]{2,1,0:T(1,128)S(1)} all-gather(f32[1,1,256]{2,1,0:T(1,128)S(1)} %bitcast.141), channel_id=1, replica_groups=mesh['dp'=16,'tensor'=2] {'dp','tensor'}, dimensions={0}, use_global_device_ids=true | all-gather | bytes 33792 | tf_op jit(solution)/shard_map/all_gather | solution.py:97
  877.4 139.7 %collective-permute-done.3 = bf16[4096,1024]{1,0:T(8,128)(2,1)} collective-permute-done((bf16[4096,1024]{1,0:T(8,128)(2,1)}, bf16[4096,1024]{1,0:T(8,128)(2,1)}, u32[]{:S(2)}, u32[]{:S(2)}) %collective-permute-start.3) | collective-permute-done | bytes 8388640 | tf_op jit(solution)/shard_map/ppermute | solution.py:17
  1040.8 42.2 %multiply_convert_fusion.1 = (bf16[704,4096]{1,0:T(8,128)(2,1)}, f32[704,4096]{1,0:T(8,128)}, f32[704,4096]{1,0:T(8,128)}) fusion(f32[4096]{0:T(1024)S(1)} %dynamic_slice.15, bf16[704,2048]{1,0:T(8,128)(2,1)} %all-gather.21.cloned.1.call-done, bf16[2048,4096]{1,0:T(8,128)(2,1)} %all-gather.23.cloned.1.call-done), kind=kOutput, calls=%fused_computation.34 | convolution fusion | flops 12001476608 | bytes 48513024 | tf_op jit(solution)/shard_map/dot_general | solution.py:158
  1083.0 27.8 %convert_reduce_fusion = (f32[4096]{0:T(1024)S(1)}, bf16[704,4096]{1,0:T(8,128)(2,1)}) fusion(f32[704,4096]{1,0:T(8,128)} %get-tuple-element.163, bf16[704,2048]{1,0:T(8,128)(2,1)} %all-gather.25.cloned.1.call-done, bf16[4096,4096]{1,0:T(8,128)(2,1)} %constant_dynamic-update-slice_fusion, s32[]{:T(128)S(6)} %select_n.32, ...), kind=kOutput, calls=%fused_computation.33 | convolution fusion | flops 11860176896 | bytes 48529412 | tf_op jit(solution)/shard_map/dot_general | solution.py:166
  1110.8 19.0 fusion.87
  1130.3 120.0 %reduce-scatter.11.cloned.1.call-done = f32[352,2048]{1,0:T(8,128)} async-done(((f32[704,2048]{1,0:T(8,128)}), f32[352,2048]{1,0:T(8,128)}) %reduce-scatter.11.cloned.1.call-update) | async-done | bytes 2883600 | tf_op jit(solution)/shard_map/reduce_scatter | solution.py:61
  1258.0 42.0 %all-gather.27.cloned.1.call-done = bf16[704,2048]{1,0:T(8,128)(2,1)} async-done(((bf16[352,2048]{1,0:T(8,128)(2,1)}), bf16[704,2048]{1,0:T(8,128)(2,1)}) %all-gather.27.cloned.1.call-update) | async-done | bytes 2883600 | tf_op jit(solution)/shard_map/all_gather | solution.py:57
  1364.0 70.3 %reduce-scatter.13.cloned.1.call-done = f32[352,2048]{1,0:T(8,128)} async-done(((f32[704,2048]{1,0:T(8,128)}), f32[352,2048]{1,0:T(8,128)}) %reduce-scatter.13.cloned.1.call-update) | async-done | bytes 2883600 | tf_op jit(solution)/shard_map/reduce_scatter | solution.py:61
  1481.1 23.2 pad_maximum_fusion.1
  1504.4 22.4 convolution_bitcast_fusion
  1526.9 19.9 fusion.88
  1546.8 45.7 %pad_maximum_fusion = f32[2048,8192]{1,0:T(8,128)} fusion(f32[2048,4096]{1,0:T(8,128)} %convolution_bitcast_fusion, f32[2048,4096]{1,0:T(8,128)} %fusion.88), kind=kLoop, calls=%fused_computation.9 | loop fusion | flops 16777216 | bytes 134217728 | tf_op jit(solution)/shard_map/concatenate | solution.py:178
  1611.4 32.7 %reduce-scatter.9.cloned.1.call-done = f32[352,2048]{1,0:T(8,128)} async-done(((f32[704,2048]{1,0:T(8,128)}), f32[352,2048]{1,0:T(8,128)}) %reduce-scatter.9.cloned.1.call-update) | async-done | bytes 2883600 | tf_op jit(solution)/shard_map/reduce_scatter | solution.py:61
  1648.0 330.8 %reduce-scatter.15.cloned.1.call-done = f32[128,4096]{1,0:T(8,128)} async-done(((f32[2048,4096]{1,0:T(8,128)}), f32[128,4096]{1,0:T(8,128)}) %reduce-scatter.15.cloned.1.call-update) | async-done | bytes 2097168 | tf_op jit(solution)/shard_map/reduce_scatter | solution.py:225
  1982.5 632.2 %reduce-scatter.17.cloned.1.call-done = f32[128,8192]{1,0:T(8,128)} async-done(((f32[2048,8192]{1,0:T(8,128)}), f32[128,8192]{1,0:T(8,128)}) %reduce-scatter.17.cloned.1.call-update) | async-done | bytes 4194320 | tf_op jit(solution)/shard_map/reduce_scatter | solution.py:177
  (326 shorter events, 297.0 us)
Async XLA Ops:
  7.3 91.4 %all-gather.11.cloned.1.call-start = ((), (), s32[]{:S(2)}) async-start(), calls=%async_computation.6 | async-start | bytes 4325376 | tf_op jit(solution)/shard_map/all_gather | solution.py:57
  54.9 335.2 %copy-start.35 = (f32[2048]{0:T(1024)}, f32[2048]{0:T(1024)S(1)}, u32[]{:S(2)}) copy-start(f32[2048]{0:T(1024)S(1)} %get-tuple-element.151) | copy-start | bytes 24580
  56.7 95.2 %all-gather.17.cloned.1.call-start = ((), (), s32[]{:S(2)}) async-start(), calls=%async_computation.9 | async-start | bytes 4456448 | tf_op jit(solution)/shard_map/all_gather | solution.py:122
  57.5 146.1 %all-gather.15.cloned.1.call-start = ((), (), s32[]{:S(2)}) async-start(), calls=%async_computation.8 | async-start | bytes 4456448 | tf_op jit(solution)/shard_map/all_gather | solution.py:121
  59.3 195.8 %all-gather.13.cloned.1.call-start = ((), (), s32[]{:S(2)}) async-start(), calls=%async_computation.7 | async-start | bytes 4456448 | tf_op jit(solution)/shard_map/all_gather | solution.py:123
  61.2 247.6 %all-gather.19.cloned.1.call-start = ((), (), s32[]{:S(2)}) async-start(), calls=%async_computation.10 | async-start | bytes 4456448 | tf_op jit(solution)/shard_map/all_gather | solution.py:124
  63.0 324.3 %reduce-scatter.7.cloned.1.call-start = ((), (), s32[]{:S(2)}) async-start(), calls=%async_computation.11 | async-start | bytes 8650752 | tf_op jit(solution)/shard_map/reduce_scatter | solution.py:61
  70.2 191.1 %copy-start.16 = (pred[704,704]{0,1:T(8,128)(4,1)}, pred[704,704]{0,1:T(8,128)(4,1)S(1)}, u32[]{:S(2)}) copy-start(pred[704,704]{0,1:T(8,128)(4,1)S(1)} %copy.89) | copy-start | bytes 1486852
  317.6 723.2 %all-gather.21.cloned.1.call-start = ((), (), s32[]{:S(2)}) async-start(), calls=%async_computation.12 | async-start | bytes 4325376 | tf_op jit(solution)/shard_map/all_gather | solution.py:57
  392.9 647.9 %all-gather.23.cloned.1.call-start = ((), (), s32[]{:S(2)}) async-start(), calls=%async_computation.13 | async-start | bytes 17825792 | tf_op jit(solution)/shard_map/all_gather | solution.py:127
  394.1 688.9 %all-gather.25.cloned.1.call-start = ((), (), s32[]{:S(2)}) async-start(), calls=%async_computation.15 | async-start | bytes 4325376 | tf_op jit(solution)/shard_map/all_gather | solution.py:57
  397.0 184.8 %copy-start.8 = (bf16[4096,128]{1,0:T(8,128)(2,1)}, bf16[4096,128]{1,0:T(8,128)(2,1)S(1)}, u32[]{:S(2)}) copy-start(bf16[4096,128]{1,0:T(8,128)(2,1)S(1)} %get-tuple-element.161) | copy-start | bytes 3145732
  397.0 15.8 collective-permute-start
  412.9 168.9 %copy-start.9 = (bf16[4096,128]{1,0:T(8,128)(2,1)}, bf16[4096,128]{1,0:T(8,128)(2,1)S(1)}, u32[]{:S(2)}) copy-start(bf16[4096,128]{1,0:T(8,128)(2,1)S(1)} %collective-permute-done) | copy-start | bytes 3145732
  413.1 57.6 %collective-permute-start.1 = (bf16[4096,256]{1,0:T(8,128)(2,1)S(1)}, bf16[4096,256]{1,0:T(8,128)(2,1)S(1)}, u32[]{:S(2)}, u32[]{:S(2)}) collective-permute-start(bf16[4096,256]{1,0:T(8,128)(2,1)S(1)} %pad_maximum_fusion.4), channel_id=1, source_target_pairs={{0,28},{2,30},{4,0},{6,2},{8,4},{10,6},{12,8},{14,10},{16,12},{18,... | collective-permute-start | bytes 6291464 | tf_op jit(solution)/shard_map/ppermute | solution.py:17
  471.1 110.7 %collective-permute-start.2 = (bf16[4096,512]{1,0:T(8,128)(2,1)S(1)}, bf16[4096,512]{1,0:T(8,128)(2,1)S(1)}, u32[]{:S(2)}, u32[]{:S(2)}) collective-permute-start(bf16[4096,512]{1,0:T(8,128)(2,1)S(1)} %pad_maximum_fusion.3), channel_id=1, source_target_pairs={{0,24},{2,26},{4,28},{6,30},{8,0},{10,2},{12,4},{14,6},{16,8},{18,... | collective-permute-start | bytes 12582920 | tf_op jit(solution)/shard_map/ppermute | solution.py:17
  586.3 430.8 %collective-permute-start.3 = (bf16[4096,1024]{1,0:T(8,128)(2,1)}, bf16[4096,1024]{1,0:T(8,128)(2,1)}, u32[]{:S(2)}, u32[]{:S(2)}) collective-permute-start(bf16[4096,1024]{1,0:T(8,128)(2,1)} %pad_maximum_fusion.2), channel_id=1, source_target_pairs={{0,16},{2,18},{4,20},{6,22},{8,24},{10,26},{12,28},{14,30},{16,0},... | collective-permute-start | bytes 25165832 | tf_op jit(solution)/shard_map/ppermute | solution.py:17
  588.6 661.7 %reduce-scatter.11.cloned.1.call-start = ((), (), s32[]{:S(2)}) async-start(), calls=%async_computation.16 | async-start | bytes 8650752 | tf_op jit(solution)/shard_map/reduce_scatter | solution.py:61
  1129.8 170.2 %all-gather.27.cloned.1.call-start = ((), (), s32[]{:S(2)}) async-start(), calls=%async_computation.17 | async-start | bytes 4325376 | tf_op jit(solution)/shard_map/all_gather | solution.py:57
  1257.9 176.4 %reduce-scatter.13.cloned.1.call-start = ((), (), s32[]{:S(2)}) async-start(), calls=%async_computation.18 | async-start | bytes 8650752 | tf_op jit(solution)/shard_map/reduce_scatter | solution.py:61
  1362.7 237.3 %all-reduce.21.cloned.1.call-start = ((), (), s32[]{:S(2)}) async-start(), calls=%async_computation.21 | async-start | bytes 212992
  1437.8 206.3 %reduce-scatter.9.cloned.1.call-start = ((), (), s32[]{:S(2)}) async-start(), calls=%async_computation.14 | async-start | bytes 8650752 | tf_op jit(solution)/shard_map/reduce_scatter | solution.py:61
  1456.8 522.0 %reduce-scatter.15.cloned.1.call-start = ((), (), s32[]{:S(2)}) async-start(), calls=%async_computation.19 | async-start | bytes 35651584 | tf_op jit(solution)/shard_map/reduce_scatter | solution.py:225
  1504.4 1110.3 %reduce-scatter.17.cloned.1.call-start = ((), (), s32[]{:S(2)}) async-start(), calls=%async_computation.20 | async-start | bytes 71303168 | tf_op jit(solution)/shard_map/reduce_scatter | solution.py:177
  (72 other events, 1886.8 us)
Sparse Core Ops, SparseCore 0:
  56.8 41.8 all-gather.10
  101.4 50.5 all-gather.16
  154.6 48.9 all-gather.14
  206.2 48.9 all-gather.12
  257.7 51.0 all-gather.18
  317.7 69.6 reduce-scatter.6
  393.0 41.9 all-gather.20
  437.2 438.3 all-gather.22
  877.2 38.7 all-gather.24
  1130.0 120.2 reduce-scatter.10
  1258.0 41.9 all-gather.26
  1362.9 71.4 reduce-scatter.12
  1441.3 128.0 all-reduce.20
  1571.6 72.4 reduce-scatter.8
  1648.2 330.5 reduce-scatter.14
  1982.9 631.7 reduce-scatter.16
